TPU v7x, 128 devices: a whole 4x4x4 slice. The times are simulated.
128 devices in a mesh: gx: 16 (over z, x_hi, core), gy: 8 (over x_lo, y).
Axes of the slice: x: 4 (x_hi: 2, x_lo: 2; x = x_hi * 2 + x_lo), y: 4, z: 4, core: 2. Of those that a mesh axis runs over, the one named last changes fastest.
Arguments:
- atom_cell: int32 [3, 16, 16, 128, 576], P(None, 'gx', 'gy'), may hold values from 0 to 7
- atom_frac: float32 [3, 16, 16, 128, 576], P(None, 'gx', 'gy'), may hold values from 0 to 1
- atom_weight: float32 [16, 16, 128, 576], P('gx', 'gy'), may hold values from 0.5 to 1.5
- block_count: int32 [16, 16, 128], P('gx', 'gy'), may hold values from 384 to 576, as said below
- miller_h: int32 [8], replicated, may hold values from 9 to 25
- miller_k: int32 [8], replicated, may hold values from 9 to 25
- miller_l: int32 [8], replicated, may hold values from 9 to 204
Outputs:
- density: float32 [128, 128, 1024], P('gx', 'gy')
- intensity: float32 [128, 256], P(('gx', 'gy'))
Inputs may be any that keep to these rules, and one draw needn't show every extreme that they name: `block_count`: slots 0 to count - 1 of a block hold its atoms; every device holds a block with exactly 576 atoms.
All inputs are finite; a program needn't handle non-finite values.
Results may differ from a plain program's by a relative error of at most 0.0023.
Values sent between devices are 32-bit elements; how exact they have to be, the bound alone decides.
A program may use at most 192 MiB of HBM per device.

v0:
```python
import math

import jax
import jax.numpy as jnp
from jax import lax
from jax.sharding import PartitionSpec as P

KERNEL_SIGMA = 0.9
NORMAL = 1.0 / (KERNEL_SIGMA * math.sqrt(2.0 * math.pi))
EXACT_DOT = lax.Precision.HIGHEST


def extended_2(cells, sides, width):
    for axis, dim in sides:
        count = lax.axis_size(axis)
        head = lax.slice_in_dim(cells, 0, width, axis=dim)
        tail = lax.slice_in_dim(cells, cells.shape[dim] - width, cells.shape[dim], axis=dim)
        cells = jnp.concatenate(
            [
                lax.ppermute(tail, axis, [(i, (i + 1) % count) for i in range(count)]),
                cells,
                lax.ppermute(head, axis, [((i + 1) % count, i) for i in range(count)]),
            ],
            axis=dim,
        )
    return cells


def kernel_taps(offsets, fraction):
    tap_rows = jnp.arange(16, dtype=jnp.int32)
    differ = tap_rows - offsets[..., None]
    inside = (differ >= 1) & (differ <= 8)
    distance = (differ - 4).astype(jnp.float32) - fraction[..., None]
    values = jnp.exp(distance * distance * (-0.5 / (KERNEL_SIGMA * KERNEL_SIGMA))) * NORMAL
    return jnp.where(inside, values, jnp.zeros_like(values))


def footprints(offsets, fraction, weights, counts):
    blocks, capacity = weights.shape
    slot_ids = jnp.arange(capacity, dtype=jnp.int32)
    occupied = (slot_ids[None, :] < counts[:, None]).astype(jnp.float32)
    taps_x = kernel_taps(offsets[0], fraction[0])
    taps_y = kernel_taps(offsets[1], fraction[1])
    taps_z = kernel_taps(offsets[2], fraction[2])
    scaled = ((weights * occupied)[..., None] * taps_z).astype(jnp.bfloat16)
    crossed = (
        (taps_x[..., :, None] * taps_y[..., None, :])
        .reshape(blocks, capacity, 256)
        .astype(jnp.bfloat16)
    )
    return jnp.einsum("bpc,bpm->bcm", scaled, crossed, preferred_element_type=jnp.float32)


def pad_along(values, along, leading, trailing):
    widths = [(0, 0)] * values.ndim
    widths[along] = (leading, trailing)
    return jnp.pad(values, widths)


def z_column(foot, depth_cells):
    nblocks = foot.shape[0]
    halves = foot.reshape(nblocks, 2, 8, 256)
    lower_half = pad_along(halves[:, 0], 0, 0, 1)
    upper_half = pad_along(halves[:, 1], 0, 1, 0)
    joined = (lower_half + upper_half).reshape((nblocks + 1) * 8, 256)
    interior = joined[4 : depth_cells + 4]
    folded = (
        interior
        + pad_along(joined[depth_cells + 4 :], 0, 0, depth_cells - 4)
        + pad_along(joined[:4], 0, depth_cells - 4, 0)
    )
    return jnp.transpose(folded, (1, 0))


def assemble(columns, blocks_x, blocks_y, depth_cells):
    pieces = columns.reshape(blocks_x, blocks_y, 2, 8, 2, 8, depth_cells)
    gathered = jnp.zeros((blocks_x + 1, blocks_y + 1, 8, 8, depth_cells), jnp.float32)
    for shift_x in range(2):
        for shift_y in range(2):
            moved = pad_along(pieces[:, :, shift_x, :, shift_y], 0, shift_x, 1 - shift_x)
            gathered = gathered + pad_along(moved, 1, shift_y, 1 - shift_y)
    gathered = jnp.transpose(gathered, (0, 2, 1, 3, 4))
    return gathered.reshape((blocks_x + 1) * 8, (blocks_y + 1) * 8, depth_cells)


def add_margins(extended, along, length):
    interior = lax.slice_in_dim(extended, 8, length + 8, axis=along)
    leading = lax.slice_in_dim(extended, 0, 4, axis=along)
    trailing = lax.slice_in_dim(extended, length + 12, length + 16, axis=along)
    return (
        interior
        + pad_along(leading, along, 0, length - 4)
        + pad_along(trailing, along, length - 4, 0)
    )


def phases(freqs, positions, extent):
    shifted = freqs[:, None] + jnp.arange(16, dtype=jnp.int32)[None, :] - 8
    product = positions[:, None, None] * shifted[None, :, :] % extent
    angles = product.astype(jnp.float32) * (2.0 * math.pi / extent)
    return (jnp.cos(angles), jnp.sin(angles))


def shards(atom_cell, atom_frac, atom_weight, block_count, miller_h, miller_k, miller_l):
    blocks_x, blocks_y, blocks_z, capacity = atom_weight.shape
    width_x = 8 * blocks_x
    width_y = 8 * blocks_y
    depth_cells = 8 * blocks_z
    columns_total = blocks_x * blocks_y
    offsets = atom_cell.reshape(3, columns_total, blocks_z, capacity)
    fraction = atom_frac.reshape(3, columns_total, blocks_z, capacity)
    weights = atom_weight.reshape(columns_total, blocks_z, capacity)
    counts = block_count.reshape(columns_total, blocks_z)

    def deposit(column_index):
        foot = footprints(
            lax.dynamic_index_in_dim(offsets, column_index, 1, False),
            lax.dynamic_index_in_dim(fraction, column_index, 1, False),
            lax.dynamic_index_in_dim(weights, column_index, 0, False),
            lax.dynamic_index_in_dim(counts, column_index, 0, False),
        )
        return z_column(foot, depth_cells)

    columns = lax.map(deposit, jnp.arange(columns_total, dtype=jnp.int32))
    padded = assemble(columns, blocks_x, blocks_y, depth_cells)
    extended = extended_2(padded, (("gx", 0),), 4)
    partway = add_margins(extended, 0, width_x)
    widened = extended_2(partway, (("gy", 1),), 4)
    density = add_margins(widened, 1, width_y)
    windows = miller_h.shape[0]
    index_x = lax.axis_index("gx")
    index_y = lax.axis_index("gy")
    total_x = width_x * lax.axis_size("gx")
    total_y = width_y * lax.axis_size("gy")
    cos_z, sin_z = phases(miller_l, jnp.arange(depth_cells, dtype=jnp.int32), depth_cells)
    table_z = jnp.concatenate([cos_z, -sin_z], axis=1).reshape(depth_cells, 2 * windows * 16)
    partial_value = jnp.dot(
        density.reshape(width_x * width_y, depth_cells),
        table_z,
        precision=EXACT_DOT,
        preferred_element_type=jnp.float32,
    )
    partial_value = partial_value.reshape(width_x, width_y, 2, windows, 16)
    part_real = partial_value[:, :, 0]
    part_imag = partial_value[:, :, 1]
    cell_y = index_y * width_y + jnp.arange(width_y, dtype=jnp.int32)
    cos_y, sin_y = phases(miller_k, cell_y, total_y)
    half_real = jnp.einsum("xywl,ywk->wxkl", part_real, cos_y, precision=EXACT_DOT) + jnp.einsum(
        "xywl,ywk->wxkl", part_imag, sin_y, precision=EXACT_DOT
    )
    half_imag = jnp.einsum("xywl,ywk->wxkl", part_imag, cos_y, precision=EXACT_DOT) - jnp.einsum(
        "xywl,ywk->wxkl", part_real, sin_y, precision=EXACT_DOT
    )
    half_real = half_real.reshape(windows, width_x, 256)
    half_imag = half_imag.reshape(windows, width_x, 256)
    cell_x = index_x * width_x + jnp.arange(width_x, dtype=jnp.int32)
    rows_here = windows * 16 // (lax.axis_size("gx") * lax.axis_size("gy"))
    row_ids = jnp.arange(rows_here * lax.axis_size(("gx", "gy")), dtype=jnp.int32)
    window_of = row_ids // 16
    shifted = jnp.take(miller_h, window_of, axis=0) + row_ids % 16 - 8
    product = shifted[:, None] * cell_x[None, :] % total_x
    angles = product.astype(jnp.float32) * (2.0 * math.pi / total_x)
    cos_x = jnp.cos(angles)
    sin_x = jnp.sin(angles)
    chosen_real = jnp.take(half_real, window_of, axis=0)
    chosen_imag = jnp.take(half_imag, window_of, axis=0)
    wave_real = jnp.einsum("rx,rxm->rm", cos_x, chosen_real, precision=EXACT_DOT) + jnp.einsum(
        "rx,rxm->rm", sin_x, chosen_imag, precision=EXACT_DOT
    )
    wave_imag = jnp.einsum("rx,rxm->rm", cos_x, chosen_imag, precision=EXACT_DOT) - jnp.einsum(
        "rx,rxm->rm", sin_x, chosen_real, precision=EXACT_DOT
    )
    summed = lax.psum_scatter(
        jnp.concatenate([wave_real, wave_imag], axis=1),
        ("gx", "gy"),
        scatter_dimension=0,
        tiled=True,
    )
    wave_real = summed[:, :256]
    wave_imag = summed[:, 256:]
    intensity = (wave_real * wave_real + wave_imag * wave_imag) / float(
        total_x * total_y * depth_cells
    )
    return (density, intensity)


def solution(mesh):
    in_specs = (
        P(None, "gx", "gy", None, None),
        P(None, "gx", "gy", None, None),
        P("gx", "gy", None, None),
        P("gx", "gy", None),
        P(),
        P(),
        P(),
    )
    out_specs = (P("gx", "gy", None), P(("gx", "gy"), None))
    return jax.shard_map(shards, mesh=mesh, in_specs=in_specs, out_specs=out_specs, check_vma=False)
```

profile of v0, /device:TPU:1, one launch (start us, length us, event | category | flops | bytes accessed | tf_op | source)
XLA Modules:
  0.0 411.3 jit_solution(15564914720105898326)
XLA Ops:
  7.2 2.9 copy.59
  10.1 2.8 copy.60
  13.2 206.0 %while.13 = (s32[]{:T(128)}, f32[2,256,1024]{2,1,0:T(8,128)}, s32[2]{0:T(128)S(1)}, s32[2,128]{1,0:T(2,128)S(1)}, f32[2,128,576]{2,1,0:T(8,128)S(1)}, /*index=5*...) while((s32[]{:T(128)}, f32[2,256,1024]{2,1,0:T(8,128)}, ...), condition=%wide.region_1.2_spmd, body=%wide.region_0.1_spmd.sunk | while | flops 683952128 | bytes 210700496 | solution.py:124
  18.2 7.0 %multiply_select_fusion.5 = (f32[128,576,16]{1,2,0:T(8,128)}, f32[128,576,16]{1,2,0:T(8,128)}) fusion(f32[128,576]{1,0:T(8,128)S(1)} %get-tuple-element.222, s32[128,576]{1,0:T(8,128)S(1)} %get-tuple-element.223, f32[128,576]{1,0:T(8,128)S(1)} %get-tuple-element.224, s32[128,576]{1,0:T(8,128)S(1)} %get-tuple-element.225), kind=kLoop, calls=%fused_computation.3.clone.1 | loop fusion | flops 25952256 | bytes 10616832 | tf_op jit(solution)/shard_map/while/body/eval_jaxpr/jit(_where)/select_n | solution.py:35
  25.2 6.1 %copy.113 = f32[128,576,16]{0,2,1:T(8,128)} copy(f32[128,576,16]{1,2,0:T(8,128)} %get-tuple-element.226) | data formatting | bytes 9437184 | tf_op jit(solution)/shard_map/while/body/eval_jaxpr/jit(_where)/select_n | solution.py:35
  31.3 6.1 %copy.114 = f32[128,576,16]{0,2,1:T(8,128)} copy(f32[128,576,16]{1,2,0:T(8,128)} %get-tuple-element.227) | data formatting | bytes 9437184 | tf_op jit(solution)/shard_map/while/body/eval_jaxpr/jit(_where)/select_n | solution.py:35
  37.4 15.4 %multiply_convert_fusion.8 = bf16[128,576,16,16]{0,3,2,1:T(8,128)(2,1)} fusion(f32[128,576,16]{0,2,1:T(8,128)} %copy.113, f32[128,576,16]{0,2,1:T(8,128)} %copy.114), kind=kLoop, calls=%fused_computation.2.clone.1 | loop fusion | flops 37748736 | bytes 47185920 | tf_op jit(solution)/shard_map/while/body/eval_jaxpr/convert_element_type | solution.py:49
  52.8 46.4 %copy.115 = bf16[128,576,256]{2,1,0:T(8,128)(2,1)} copy(bf16[128,576,256]{0,2,1:T(8,128)(2,1)} %bitcast.156) | data formatting | bytes 75497472 | tf_op jit(solution)/shard_map/while/body/eval_jaxpr/convert_element_type | solution.py:49
  99.3 15.0 %fusion.126 = f32[128,2,8,256]{3,2,1,0:T(8,128)S(1)} fusion(bf16[128,576,256]{2,1,0:T(8,128)(2,1)} %copy.115, f32[128,576]{1,0:T(8,128)S(1)} %get-tuple-element.228, s32[128,576]{1,0:T(8,128)S(1)} %get-tuple-element.229, f32[128,576]{1,0:T(8,128)S(1)} %bitcast_select_fusion.3), kind=kOutput, calls=%fused_computation.28.clone.1 | convolution fusion | flops 619315200 | bytes 40730624 | tf_op jit(solution)/shard_map/while/body/eval_jaxpr/bpc,bpm->bcm/dot_general | solution.py:51
  121.2 7.0 %multiply_select_fusion.5 = (f32[128,576,16]{1,2,0:T(8,128)}, f32[128,576,16]{1,2,0:T(8,128)}) fusion(f32[128,576]{1,0:T(8,128)S(1)} %get-tuple-element.222, s32[128,576]{1,0:T(8,128)S(1)} %get-tuple-element.223, f32[128,576]{1,0:T(8,128)S(1)} %get-tuple-element.224, s32[128,576]{1,0:T(8,128)S(1)} %get-tuple-element.225), kind=kLoop, calls=%fused_computation.3.clone.1 | loop fusion | flops 25952256 | bytes 10616832 | tf_op jit(solution)/shard_map/while/body/eval_jaxpr/jit(_where)/select_n | solution.py:35
  128.2 6.1 %copy.113 = f32[128,576,16]{0,2,1:T(8,128)} copy(f32[128,576,16]{1,2,0:T(8,128)} %get-tuple-element.226) | data formatting | bytes 9437184 | tf_op jit(solution)/shard_map/while/body/eval_jaxpr/jit(_where)/select_n | solution.py:35
  134.3 6.1 %copy.114 = f32[128,576,16]{0,2,1:T(8,128)} copy(f32[128,576,16]{1,2,0:T(8,128)} %get-tuple-element.227) | data formatting | bytes 9437184 | tf_op jit(solution)/shard_map/while/body/eval_jaxpr/jit(_where)/select_n | solution.py:35
  140.4 15.4 %multiply_convert_fusion.8 = bf16[128,576,16,16]{0,3,2,1:T(8,128)(2,1)} fusion(f32[128,576,16]{0,2,1:T(8,128)} %copy.113, f32[128,576,16]{0,2,1:T(8,128)} %copy.114), kind=kLoop, calls=%fused_computation.2.clone.1 | loop fusion | flops 37748736 | bytes 47185920 | tf_op jit(solution)/shard_map/while/body/eval_jaxpr/convert_element_type | solution.py:49
  155.8 46.4 %copy.115 = bf16[128,576,256]{2,1,0:T(8,128)(2,1)} copy(bf16[128,576,256]{0,2,1:T(8,128)(2,1)} %bitcast.156) | data formatting | bytes 75497472 | tf_op jit(solution)/shard_map/while/body/eval_jaxpr/convert_element_type | solution.py:49
  202.3 15.0 %fusion.126 = f32[128,2,8,256]{3,2,1,0:T(8,128)S(1)} fusion(bf16[128,576,256]{2,1,0:T(8,128)(2,1)} %copy.115, f32[128,576]{1,0:T(8,128)S(1)} %get-tuple-element.228, s32[128,576]{1,0:T(8,128)S(1)} %get-tuple-element.229, f32[128,576]{1,0:T(8,128)S(1)} %bitcast_select_fusion.3), kind=kOutput, calls=%fused_computation.28.clone.1 | convolution fusion | flops 619315200 | bytes 40730624 | tf_op jit(solution)/shard_map/while/body/eval_jaxpr/bpc,bpm->bcm/dot_general | solution.py:51
  219.2 1.7 slice_bitcast_fusion.7
  221.3 4.2 %collective-permute-start = (f32[4,24,1024]{2,1,0:T(8,128)S(1)}, f32[4,24,1024]{2,1,0:T(8,128)S(1)}, u32[]{:S(2)}, u32[]{:S(2)}) collective-permute-start(f32[4,24,1024]{2,1,0:T(8,128)S(1)} %get-tuple-element.147), channel_id=1, source_target_pairs={{0,8},{8,16},{16,24},{24,32},{32,40},{40,48},{48,56},{56,64},{64,7... | collective-permute-start | bytes 1179656 | tf_op jit(solution)/shard_map/ppermute | solution.py:20
  226.4 5.2 %fusion.86 = s32[128]{0:T(128)S(1)} fusion(s32[]{:T(128)} %bitcast.29, s32[]{:T(128)} %bitcast.30, s32[]{:T(128)} %bitcast.31, s32[]{:T(128)} %bitcast.32, s32[]{:T(128)} %bitcast.33, s32[]{:T(128)} %bitcast.35, s32[]{:T(128)} %bitcast.34, s32[]{:T(128)} %bitcast.28), kind=kLoop, calls=%fused_computation.160 | loop fusion | flops 5888 | bytes 544 | tf_op jit(solution)/shard_map/sub | solution.py:160
  231.9 2.1 fusion.64
  234.1 2.4 collective-permute-done.1
  238.0 2.4 collective-permute-start.3
  240.6 2.2 collective-permute-done.2
  242.9 3.8 fusion.45
  257.5 145.6 %all-reduce.19.cloned.1.call-done = f32[128,512]{1,0:T(8,128)} async-done(((f32[128,512]{1,0:T(8,128)}), f32[128,512]{1,0:T(8,128)}) %all-reduce.19.cloned.1.call-update) | async-done | bytes 262160
  (75 shorter events, 25.7 us)
Async XLA Ops:
  7.2 5.8 %copy-start = (f32[1,2,128,576]{2,3,1,0:T(8,128)S(1)}, f32[1,2,128,576]{2,3,1,0:T(8,128)}, u32[]{:S(2)}) copy-start(f32[1,2,128,576]{2,3,1,0:T(8,128)} %param.13) | copy-start | bytes 1769476
  7.2 6.0 %copy-start.5 = (s32[1,2,128]{2,1,0:T(2,128)S(1)}, s32[1,2,128]{2,1,0:T(2,128)}, u32[]{:S(2)}) copy-start(s32[1,2,128]{2,1,0:T(2,128)} %param.14) | copy-start | bytes 3076
  7.2 396.0 %all-reduce.19.cloned.1.call-start = ((), (), s32[]{:S(2)}) async-start(), calls=%async_computation | async-start | bytes 524288
  220.8 4.7 %copy-start.3 = (s32[8]{0:T(128)S(1)}, s32[8]{0:T(128)}, u32[]{:S(2)}) copy-start(s32[8]{0:T(128)} %param.17) | copy-start | bytes 100
  220.8 4.8 %copy-start.4 = (s32[8]{0:T(128)S(1)}, s32[8]{0:T(128)}, u32[]{:S(2)}) copy-start(s32[8]{0:T(128)} %param.16) | copy-start | bytes 100
  220.8 4.9 %copy-start.2 = (s32[8]{0:T(128)S(1)}, s32[8]{0:T(128)}, u32[]{:S(2)}) copy-start(s32[8]{0:T(128)} %param.15) | copy-start | bytes 100
  221.3 12.7 %collective-permute-start = (f32[4,24,1024]{2,1,0:T(8,128)S(1)}, f32[4,24,1024]{2,1,0:T(8,128)S(1)}, u32[]{:S(2)}, u32[]{:S(2)}) collective-permute-start(f32[4,24,1024]{2,1,0:T(8,128)S(1)} %get-tuple-element.147), channel_id=1, source_target_pairs={{0,8},{8,16},{16,24},{24,32},{32,40},{40,48},{48,56},{56,64},{64,7... | collective-permute-start | bytes 1179656 | tf_op jit(solution)/shard_map/ppermute | solution.py:20
  225.5 11.0 %collective-permute-start.1 = (f32[4,24,1024]{2,1,0:T(8,128)S(1)}, f32[4,24,1024]{2,1,0:T(8,128)S(1)}, u32[]{:S(2)}, u32[]{:S(2)}) collective-permute-start(f32[4,24,1024]{2,1,0:T(8,128)S(1)} %get-tuple-element.148), channel_id=1, source_target_pairs={{8,0},{16,8},{24,16},{32,24},{40,32},{48,40},{56,48},{64,56},{72,6... | collective-permute-start | bytes 1179656 | tf_op jit(solution)/shard_map/ppermute | solution.py:22
  236.7 6.1 %collective-permute-start.2 = (f32[8,4,1024]{2,1,0:T(4,128)S(1)}, f32[8,4,1024]{2,1,0:T(4,128)S(1)}, u32[]{:S(2)}, u32[]{:S(2)}) collective-permute-start(f32[8,4,1024]{2,1,0:T(4,128)S(1)} %get-tuple-element.151), channel_id=1, source_target_pairs={{0,1},{1,2},{2,3},{3,4},{4,5},{5,6},{6,7},{7,0},{8,9},{9,10},{10,1... | collective-permute-start | bytes 393224 | tf_op jit(solution)/shard_map/ppermute | solution.py:20
  238.0 4.7 %collective-permute-start.3 = (f32[8,4,1024]{2,1,0:T(4,128)S(1)}, f32[8,4,1024]{2,1,0:T(4,128)S(1)}, u32[]{:S(2)}, u32[]{:S(2)}) collective-permute-start(f32[8,4,1024]{2,1,0:T(4,128)S(1)} %get-tuple-element.152), channel_id=1, source_target_pairs={{1,0},{2,1},{3,2},{4,3},{5,4},{6,5},{7,6},{0,7},{9,8},{10,9},{11,1... | collective-permute-start | bytes 393224 | tf_op jit(solution)/shard_map/ppermute | solution.py:22
  242.9 7.5 %copy-start.1 = (f32[8,16,1024]{2,1,0:T(8,128)}, f32[8,16,1024]{2,1,0:T(8,128)S(1)}, u32[]{:S(2)}) copy-start(f32[8,16,1024]{2,1,0:T(8,128)S(1)} %fusion.44) | copy-start | bytes 1572868
Sparse Core Ops, SparseCore 0:
  257.7 145.4 all-reduce.18
where the time goes:
time: 414 us; the launch traced here: 411 us
  waiting for transfers between devices  150 us (36%)
  local copies, waits for them, and re-layouts  137 us (33%)
  other arithmetic  55.8 us (13%)
  matrix products  41.7 us (10%)
  between operations  14.3 us (3%)
  starting transfers between devices  8.04 us (2%)
    unnamed x2, waiting for transfers between devices  146 us
    convert_element_type x2, local copies, waits for them, and re-layouts, footprints(): crossed = (taps_x[..., :, None] * taps_y[..., None, :]).reshape(blocks, c...  92.8 us
    convert_element_type x2, other arithmetic, footprints(): crossed = (taps_x[..., :, None] * taps_y[..., None, :]).reshape(blocks, c...  30.8 us
    dot_general x2, matrix products, footprints(): jnp.einsum('bpc,bpm->bcm', scaled, crossed, preferred_element_type=jnp.fl...  30 us
    select_n x4, local copies, waits for them, and re-layouts, kernel_taps(): return jnp.where(inside, values, jnp.zeros_like(values))  24.4 us
    select_n x2, other arithmetic, kernel_taps(): return jnp.where(inside, values, jnp.zeros_like(values))  13.9 us
  transfers between devices with their start and end apart: 5, of which 3 were waited for; matrix products, arithmetic and copies ran while one was open for 2% of the time, Pallas kernels for 0%

commit v1 on v0

v1 whole, which is shorter than its diff:
```python
import math
import jax, jax.numpy as jnp
from jax import lax
from jax.experimental import pallas as pl
from jax.experimental.pallas import tpu as pltpu
from jax.sharding import PartitionSpec as P

SIGMA2 = 0.9 * 0.9
INV = 1.0 / SIGMA2
NORMAL = 1.0 / (0.9 * math.sqrt(2.0 * math.pi))
F32 = jnp.float32
BF16 = jnp.bfloat16
NT = (((1,), (1,)), ((), ()))
NN = (((1,), (0,)), ((), ()))


def iota(shape, dim):
    return lax.broadcasted_iota(jnp.int32, shape, dim)


def slot(row):
    return row - 4 if row >= 4 else row + 12


def dense_taps(cell, frac, scale, out, buf, tile):
    u = cell.astype(F32) + (frac - 4.0)
    up = jnp.exp(u * INV)
    down = jnp.exp(u * (-INV))
    mid = jnp.exp(u * u * (-0.5 * INV)) * scale
    out[buf, tile, 32:40, :] = mid
    for sign, ratio in ((1, up), (-1, down)):
        p = mid
        for k in range(1, 8):
            p = p * (ratio * math.exp(-(2 * k - 1) * 0.5 * INV))
            r = slot(8 + sign * k)
            keep = cell >= k if sign > 0 else cell <= 7 - k
            out[buf, tile, 8 * r : 8 * r + 8, :] = jnp.where(keep, p, 0.0)


def crossed(x, y, buf, tile, b):
    yy = y[buf, tile, pl.ds(b, 16, stride=8), :].astype(BF16)
    parts = []
    for a in range(16):
        if a == 12:
            parts.append(jnp.zeros((16, 128), BF16))
            continue
        x8 = x[buf, tile, pl.ds(a * 8 + b, 8, stride=0), :]
        parts.append(jnp.concatenate([x8, x8], 0).astype(BF16) * yy)
    return jnp.concatenate(parts, 0)


def sincos(q, extent):
    eighth = extent // 8
    s = q + eighth
    quad = (s >> (extent.bit_length() - 3)) & 3
    r = ((s & (2 * eighth - 1)) - eighth).astype(F32) * (2.0 * math.pi / extent)
    r2 = r * r
    sin = r * (1.0 + r2 * (-1 / 6 + r2 * (1 / 120 + r2 * (-1 / 5040 + r2 * (1 / 362880)))))
    cos = 1.0 + r2 * (-0.5 + r2 * (1 / 24 + r2 * (-1 / 720 + r2 * (1 / 40320 + r2 * (-1 / 3628800)))))
    odd = (quad & 1) == 1
    c = jnp.where(odd, sin, cos)
    s = jnp.where(odd, cos, sin)
    c = jnp.where((quad == 1) | (quad == 2), -c, c)
    s = jnp.where(quad >= 2, -s, s)
    return c, s


def split(v):
    hi = v.astype(BF16)
    return hi, (v - hi.astype(F32)).astype(BF16)


def mm(a, b, dims=NN):
    return lax.dot_general(a, b, dims, preferred_element_type=F32)


def local_kernel(
    cnt, cell, frac, w, mh, mk, ml,
    y_out, up_out, down_out, r_out,
    packed, fx, fy, fz, ws, xs, ys, zs, inner, edge, tab_hi, tab_lo, zsum, tt, d_hi, d_lo,
):
    def pieces(fn, out):
        for t in range(9):
            if t < 8:
                v = fn(t // 4, 128 * (t % 4), 128)
            else:
                v = jnp.concatenate([fn(0, 512, 64), fn(1, 512, 64)], 0)
            out[t] = v.T

    pieces(lambda c, s, n: cell[0, c, s : s + n] + cell[1, c, s : s + n] * 8 + cell[2, c, s : s + n] * 64, packed)
    for d, o in ((0, fx), (1, fy), (2, fz)):
        pieces(lambda c, s, n: frac[d, c, s : s + n], o)

    def weigh(c, s, n):
        return jnp.where(iota((n, 128), 0) + s < cnt[c : c + 1, :], w[c, s : s + n] * NORMAL, 0.0)

    pieces(weigh, ws)
    for o in (ys, zs):
        for buf in range(2):
            for t in range(9):
                o[buf, t, 96:104, :] = jnp.zeros((8, 128), F32)

    def dense(g, buf):
        gs = pl.ds(pl.multiple_of(g * 8, 8), 8)
        for t in range(9):
            q = packed[t, gs, :]
            dense_taps(q & 7, fx[t, gs, :], NORMAL, xs, buf, t)
            dense_taps((q >> 3) & 7, fy[t, gs, :], NORMAL, ys, buf, t)
            dense_taps(q >> 6, fz[t, gs, :], ws[t, gs, :], zs, buf, t)

    dense(0, 0)
    lane16 = iota((16, 128), 1)

    def group(g, _):
        buf = g & 1
        for b in range(8):
            zt = zs[buf, 8, pl.ds(b, 16, stride=8), :]
            zm = jnp.concatenate([jnp.where(lane16 < 64, zt, 0.0), jnp.where(lane16 < 64, 0.0, zt)], 0).astype(BF16)
            fm = mm(zm, crossed(xs, ys, buf, 8, b), NT)
            for c in range(2):
                f = fm[16 * c : 16 * c + 16]
                for t in (4 * c, 4 * c + 2):
                    zz = jnp.concatenate([zs[buf, t + e, pl.ds(b, 16, stride=8), :] for e in (0, 1)], 1).astype(BF16)
                    cc = jnp.concatenate([crossed(xs, ys, buf, t + e, b) for e in (0, 1)], 1)
                    f = f + mm(zz, cc, NT)
                base = pl.multiple_of(g * 64 + b * 8, 8)
                inner[c, pl.ds(base, 8), :] = f[0:8]
                edge[c, pl.ds(base + 8, 8), :] = f[8:16]
        dense(jnp.minimum(g + 1, 15), 1 - buf)
        return 0

    lax.fori_loop(0, 16, group, 0)
    for c in range(2):
        edge[c, 0:8, :] = edge[c, 1024:1032, :]
        edge[c, 1032:1040, :] = edge[c, 8:16, :]

    row8 = iota((8, 128), 0)
    lane8 = iota((8, 128), 1)
    ls = [ml[v // 2] + (row8 + 8 * (v % 2) - 8) for v in range(16)]
    lcol = jnp.concatenate(ls, 0)
    zl = iota((128, 128), 1)
    c0, s0 = sincos((lcol * zl) & 1023, 1024)
    cw, sw = sincos((lcol * 128) & 1023, 1024)
    for t in range(8):
        for half, v in ((0, c0), (1, -s0)):
            hi, lo = split(v)
            tab_hi[128 * half : 128 * half + 128, 128 * t : 128 * t + 128] = hi
            tab_lo[128 * half : 128 * half + 128, 128 * t : 128 * t + 128] = lo
        c0, s0 = c0 * cw - s0 * sw, s0 * cw + c0 * sw

    low256 = (iota((256, 256), 0) & 7) < 4
    for c in range(2):
        def ztile(t, _, c=c):
            zs0 = pl.multiple_of(t * 256, 256)
            d = inner[c, pl.ds(zs0, 256), :] + jnp.where(
                low256, edge[c, pl.ds(zs0, 256), :], edge[c, pl.ds(zs0 + 16, 256), :]
            )
            tt[c, :, pl.ds(zs0, 256)] = d.T
            hi, lo = split(d)
            d_hi[...] = hi
            d_lo[...] = lo
            th = tab_hi[:, pl.ds(zs0, 256)]
            tl = tab_lo[:, pl.ds(zs0, 256)]
            part = mm(th, d_hi[...]) + mm(th, d_lo[...]) + mm(tl, d_hi[...])

            @pl.when(t == 0)
            def _():
                zsum[c] = part

            @pl.when(t > 0)
            def _():
                zsum[c] += part

            return 0

        lax.fori_loop(0, 4, ztile, 0)

    low = iota((8, 1024), 0) < 4
    for k in range(8):
        tops, bottoms = [], []
        for a in (2 * k, 2 * k + 1):
            in0, out0 = tt[0, 16 * a : 16 * a + 8, :], tt[0, 16 * a + 8 : 16 * a + 16, :]
            in1, out1 = tt[1, 16 * a : 16 * a + 8, :], tt[1, 16 * a + 8 : 16 * a + 16, :]
            y_out[a, 0:8, :] = in0 + jnp.where(low, 0.0, out1)
            y_out[a, 8:16, :] = in1 + jnp.where(low, out0, 0.0)
            tops.append(out1)
            bottoms.append(out0)
        up_out[k] = jnp.where(low, tops[0], pltpu.roll(tops[1], 4, 0))
        down_out[k] = jnp.where(low, pltpu.roll(bottoms[0], 4, 0), bottoms[1])

    x0 = lax.axis_index("gx") * 8
    y0 = lax.axis_index("gy") * 16
    n = iota((16, 256), 1)
    ip = (n & 63) >> 2
    ni = (ip & 1) * 8 + (ip >> 1) - 8
    nj = (n >> 6) * 4 + (n & 3) - 8
    off = iota((16, 256), 0)
    off = jnp.where(off < 12, off, off - 16)
    lane_low = iota((16, 128), 1) < 64

    def pair(v, _):
        us = []
        for e in range(2):
            win = 2 * v + e
            hx = mh[win] + ni
            ky = mk[win] + nj
            xr, xi = sincos((hx * (x0 + off)) & 127, 128)
            yr, yi = sincos((ky * (y0 + off)) & 127, 128)
            pr, pi = sincos((ky[0:1] * 8) & 127, 128)
            mr, mi = [], []
            for a in range(16):
                mr.append(xr[a : a + 1] * yr - xi[a : a + 1] * yi)
                mi.append(-(xr[a : a + 1] * yi + xi[a : a + 1] * yr))
            mr = jnp.concatenate(mr, 0)
            mi = jnp.concatenate(mi, 0)
            mrh, mrl = split(mr)
            mih, mil = split(mi)
            rows = [
                zsum[c, pl.ds(pl.multiple_of(128 * half + win * 16, 16), 16), :] for c in (0, 1) for half in (0, 1)
            ]
            zh, zl_ = split(jnp.concatenate(rows, 0))
            A = mm(zh, mrh) + mm(zl_, mrh) + mm(zh, mrl)
            B = mm(zh, mih) + mm(zl_, mih) + mm(zh, mil)
            re0, im0 = A[0:16] - B[16:32], A[16:32] + B[0:16]
            re1, im1 = A[32:48] - B[48:64], A[48:64] + B[32:48]
            re = re0 + re1 * pr + im1 * pi
            im = im0 + im1 * pr - re1 * pi
            us.append((re, im))
        rows = []
        for jh in range(4):
            for part in range(2):
                a0 = us[0][part][:, 128 * (jh // 2) : 128 * (jh // 2) + 128]
                a1 = us[1][part][:, 128 * (jh // 2) : 128 * (jh // 2) + 128]
                if jh % 2 == 0:
                    rows.append(jnp.where(lane_low, a0, pltpu.roll(a1, 64, 1)))
                else:
                    rows.append(jnp.where(lane_low, pltpu.roll(a0, 64, 1), a1))
        tr = jnp.concatenate(rows, 0).T
        for e in range(2):
            for il in range(8):
                r_out[il, 2 * v + e] = tr[64 * e + 8 * il : 64 * e + 8 * il + 8]
        return 0

    lax.fori_loop(0, 4, pair, 0)


def local(cell, frac, w, cnt, mh, mk, ml):
    cell = jnp.swapaxes(cell, 2, 3)
    frac = jnp.swapaxes(frac, 2, 3)
    w = jnp.swapaxes(w, 1, 2)
    vm = pl.BlockSpec(memory_space=pltpu.VMEM)
    sm = pl.BlockSpec(memory_space=pltpu.SMEM)
    sd = jax.ShapeDtypeStruct
    return pl.pallas_call(
        local_kernel,
        out_shape=(sd((16, 16, 1024), F32), sd((8, 8, 1024), F32), sd((8, 8, 1024), F32), sd((8, 8, 8, 128), F32)),
        in_specs=[vm] * 4 + [sm] * 3,
        out_specs=(vm,) * 4,
        scratch_shapes=[pltpu.VMEM((9, 128, 128), jnp.int32)]
        + [pltpu.VMEM((9, 128, 128), F32)] * 4
        + [pltpu.VMEM((2, 9, 128, 128), F32)] * 3
        + [
            pltpu.VMEM((2, 1024, 256), F32),
            pltpu.VMEM((2, 1040, 256), F32),
            pltpu.VMEM((256, 1024), BF16),
            pltpu.VMEM((256, 1024), BF16),
            pltpu.VMEM((2, 256, 256), F32),
            pltpu.VMEM((2, 256, 1024), F32),
            pltpu.VMEM((256, 256), BF16),
            pltpu.VMEM((256, 256), BF16),
        ],
        compiler_params=pltpu.CompilerParams(vmem_limit_bytes=60 * 2**20),
    )(cnt, cell, frac, w, mh, mk, ml)


MESH = pl.DeviceIdType.MESH
CHUNK = 256


def exchange_kernel(
    y_in, up_in, down_in, r_in, dens, inten,
    q, up_got, down_got, left_got, right_got, got1, part, got2,
    s1, g1, s2, g2, up_s, up_g, down_s, down_g, right_s, right_g, left_s, left_g,
):
    nx, ny = lax.axis_size("gx"), lax.axis_size("gy")
    me_x, me_y = lax.axis_index("gx"), lax.axis_index("gy")
    barrier = pltpu.get_barrier_semaphore()

    def greet_y(d, _):
        pl.semaphore_signal(barrier, inc=1, device_id=(me_x, (me_y + d) % ny), device_id_type=MESH)
        return 0

    def greet_x(d, _):
        pl.semaphore_signal(barrier, inc=1, device_id=((me_x + d) % nx, me_y), device_id_type=MESH)
        return 0

    lax.fori_loop(1, ny, greet_y, 0)
    lax.fori_loop(1, nx, greet_x, 0)
    pl.semaphore_wait(barrier, nx + ny - 2)

    def first(d):
        to = (me_y + d) % ny
        return pltpu.make_async_remote_copy(
            r_in.at[to], got1.at[d], s1.at[d], g1.at[d], device_id=(me_x, to), device_id_type=MESH
        )

    def second(d):
        to = (me_x + d) % nx
        return pltpu.make_async_remote_copy(
            part.at[to // 2], got2.at[d], s2.at[d], g2.at[d], device_id=(to, me_y), device_id_type=MESH
        )

    def piece(src, dst, ss, gs, c, to):
        z = pl.ds(c * CHUNK, CHUNK)
        return pltpu.make_async_remote_copy(
            src.at[:, :, z], dst.at[:, :, z], ss.at[c], gs.at[c], device_id=to, device_id_type=MESH
        )

    up = lambda c: piece(up_in, up_got, up_s, up_g, c, (me_x, (me_y + 1) % ny))
    down = lambda c: piece(down_in, down_got, down_s, down_g, c, (me_x, (me_y + ny - 1) % ny))
    right = lambda c: piece(q.at[pl.ds(8, 4)], right_got, right_s, right_g, c, ((me_x + 1) % nx, me_y))
    left = lambda c: piece(q.at[pl.ds(12, 4)], left_got, left_s, left_g, c, ((me_x + nx - 1) % nx, me_y))

    def start(copy):
        def body(i, _):
            copy(i).start()
            return 0

        return body

    def finish(copy):
        def body(i, _):
            copy(i).wait()
            return 0

        return body

    lax.fori_loop(1, ny, start(first), 0)
    for c in range(4):
        up(c).start()
        down(c).start()

    low = iota((8, CHUNK), 0) < 4
    for c in range(4):
        z = slice(c * CHUNK, c * CHUNK + CHUNK)
        up(c).wait()
        down(c).wait()
        for k in (4, 5, 6, 7, 0, 1, 2, 3):
            a = 2 * k
            u, d = up_got[k, :, z], down_got[k, :, z]
            q[a, 0:8, z] = y_in[a, 0:8, z] + jnp.where(low, u, 0.0)
            q[a + 1, 0:8, z] = y_in[a + 1, 0:8, z] + jnp.where(low, pltpu.roll(u, 4, 0), 0.0)
            q[a, 8:16, z] = y_in[a, 8:16, z] + jnp.where(low, 0.0, pltpu.roll(d, 4, 0))
            q[a + 1, 8:16, z] = y_in[a + 1, 8:16, z] + jnp.where(low, 0.0, d)
        right(c).start()
        left(c).start()

    lax.fori_loop(1, ny, finish(first), 0)
    part[...] = r_in[me_y] + lax.fori_loop(2, ny, lambda d, t: t + got1[d], got1[1])
    lax.fori_loop(1, nx, start(second), 0)
    lax.fori_loop(1, nx, finish(second), 0)
    total = part[me_x // 2] + lax.fori_loop(2, nx, lambda d, t: t + got2[d], got2[1])
    mine = jnp.where((iota((8, 128), 0) * 0 + me_x % 2) == 1, pltpu.roll(total, 4, 0), total)
    power = mine * mine
    power = power + pltpu.roll(power, 112, 1)
    n = iota((128, 256), 1)
    pick = (iota((128, 256), 0) == (n >> 6) * 32 + (n & 15)).astype(F32)
    wide = lax.dot_general(power, pick, NN, precision=lax.Precision.HIGHEST, preferred_element_type=F32)
    keep = iota((8, 256), 0) == ((iota((8, 256), 1) >> 4) & 3)
    inten[...] = jnp.sum(jnp.where(keep, wide, 0.0), axis=0, keepdims=True) * (1.0 / 16777216.0)

    for c in range(4):
        z = slice(c * CHUNK, c * CHUNK + CHUNK)
        right(c).wait()
        left(c).wait()
        dens[0:4, :, z] = q[0:4, :, z] + right_got[:, :, z]
        dens[4:8, :, z] = q[4:8, :, z] + left_got[:, :, z]


def exchange(y, up, down, r):
    vm = pl.BlockSpec(memory_space=pltpu.VMEM)
    sd = jax.ShapeDtypeStruct
    dma = pltpu.SemaphoreType.DMA
    return pl.pallas_call(
        exchange_kernel,
        out_shape=(sd((8, 16, 1024), F32), sd((1, 256), F32)),
        in_specs=[vm] * 4,
        out_specs=(vm, vm),
        scratch_shapes=[
            pltpu.VMEM((16, 16, 1024), F32),
            pltpu.VMEM((8, 8, 1024), F32),
            pltpu.VMEM((8, 8, 1024), F32),
            pltpu.VMEM((4, 16, 1024), F32),
            pltpu.VMEM((4, 16, 1024), F32),
            pltpu.VMEM((8, 8, 8, 128), F32),
            pltpu.VMEM((8, 8, 128), F32),
            pltpu.VMEM((16, 8, 128), F32),
            dma((8,)), dma((8,)), dma((16,)), dma((16,)),
        ]
        + [dma((4,))] * 8,
        compiler_params=pltpu.CompilerParams(
            collective_id=0, has_side_effects=True, vmem_limit_bytes=40 * 2**20
        ),
    )(y, up, down, r)


def shards(atom_cell, atom_frac, atom_weight, block_count, miller_h, miller_k, miller_l):
    y, up, down, r = local(
        atom_cell[:, 0], atom_frac[:, 0], atom_weight[0], block_count[0], miller_h, miller_k, miller_l
    )
    return exchange(y, up, down, r)


def solution(mesh):
    in_specs = (
        P(None, "gx", "gy", None, None),
        P(None, "gx", "gy", None, None),
        P("gx", "gy", None, None),
        P("gx", "gy", None),
        P(),
        P(),
        P(),
    )
    out_specs = (P("gx", "gy", None), P(("gx", "gy"), None))
    return jax.shard_map(shards, mesh=mesh, in_specs=in_specs, out_specs=out_specs, check_vma=False)
```

time: 414 us -> 70 us (0.17)
  waiting for transfers between devices: 150 us -> 0 us
  local copies, waits for them, and re-layouts: 137 us -> 5.43 us
  Pallas kernels: 0 us -> 63.6 us
  other arithmetic: 55.8 us -> 0 us
  matrix products: 41.7 us -> 0 us
  between operations: 14.3 us -> 0.65 us
  starting transfers between devices: 8.04 us -> 0 us
    unnamed x2 -> x0, waiting for transfers between devices: 146 us -> none
    convert_element_type x2 -> x0, local copies, waits for them, and re-layouts: 92.8 us -> none  [footprints(): crossed = (taps_x[..., :, None] * taps_y[..., None, :]).reshape(blocks, c...]
    pallas_call x0 -> x2, Pallas kernels: none -> 63.6 us  [the longest x1 36.2 us: local(): pl.pallas_call(local_kernel, out_shape=(sd((16, 16, 1024), F32), sd((8, 8...]
    dot_general x11 -> x0, matrix products: 41.7 us -> none  [the longest x2 30 us: footprints(): jnp.einsum('bpc,bpm->bcm', scaled, crossed, preferred_element_type=jnp.fl...]
    convert_element_type x2 -> x0, other arithmetic: 30.8 us -> none  [footprints(): crossed = (taps_x[..., :, None] * taps_y[..., None, :]).reshape(blocks, c...]
    select_n x4 -> x0, local copies, waits for them, and re-layouts: 24.4 us -> none  [kernel_taps(): return jnp.where(inside, values, jnp.zeros_like(values))]
    select_n x3 -> x0, other arithmetic: 13.9 us -> none  [the longest x2 13.9 us: kernel_taps(): return jnp.where(inside, values, jnp.zeros_like(values))]
    ppermute x4 -> x0, starting transfers between devices: 8 us -> none  [the longest x2 5.56 us: extended_2(): lax.ppermute(tail, axis, [(i, (i + 1) % count) for i in range(count)])]
  transfers between devices with their start and end apart: 5 -> 0, of which waited for: 3 -> 0; matrix products, arithmetic and copies ran while one was open for 2% -> 0% of each run, Pallas kernels for 0% -> 0%
where the time goes in v1:
time: 70 us; the launch traced here: 69.7 us
  Pallas kernels  63.6 us (91%)
  local copies, waits for them, and re-layouts  5.43 us (8%)
    pallas_call x1, Pallas kernels, local(): pl.pallas_call(local_kernel, out_shape=(sd((16, 16, 1024), F32), sd((8, 8...  36.2 us
    pallas_call x1, Pallas kernels, exchange(): pl.pallas_call(exchange_kernel, out_shape=(sd((8, 16, 1024), F32), sd((1,...  27.5 us
    unnamed x10, local copies, waits for them, and re-layouts  5.43 us

profile of v1, /device:TPU:1, one launch (start us, length us, event | category | flops | bytes accessed | tf_op | source)
XLA Modules:
  0.0 69.7 jit_solution(10902084375428973289)
XLA Ops:
  0.6 36.2 %shard_map.86 = (f32[16,16,1024]{2,1,0:T(8,128)}, f32[8,8,1024]{2,1,0:T(8,128)}, f32[8,8,1024]{2,1,0:T(8,128)}, f32[8,8,8,128]{3,2,1,0:T(8,128)}) custom-call(s32[2,128]{1,0:T(2,128)} %bitcast.13, s32[3,2,576,128]{3,2,1,0:T(8,128)} %bitcast.10, f32[3,2,576,128]{3,2,1,0:T(8,128)} %bitcast.11, f32[2,576,128]{2,1,0:T(8,128)} %bitcast.12, s32[8]{0:T(128)} %mh.1, ...), custom_call_target="tpu_custom_call" | custom-call | tf_op jit(solution)/shard_map/pallas_call | solution.py:254
  36.8 0.0 copy-start
  36.8 1.2 %copy-done = f32[16,16,1024]{2,1,0:T(8,128)S(1)} copy-done((f32[16,16,1024]{2,1,0:T(8,128)S(1)}, f32[16,16,1024]{2,1,0:T(8,128)}, u32[]{:S(2)}) %copy-start) | copy-done | bytes 1048600
  38.0 0.0 copy-start.1
  38.0 0.9 %copy-done.1 = f32[8,8,1024]{2,1,0:T(8,128)S(1)} copy-done((f32[8,8,1024]{2,1,0:T(8,128)S(1)}, f32[8,8,1024]{2,1,0:T(8,128)}, u32[]{:S(2)}) %copy-start.1) | copy-done | bytes 262168
  39.0 0.0 copy-start.2
  39.0 0.9 %copy-done.2 = f32[8,8,1024]{2,1,0:T(8,128)S(1)} copy-done((f32[8,8,1024]{2,1,0:T(8,128)S(1)}, f32[8,8,1024]{2,1,0:T(8,128)}, u32[]{:S(2)}) %copy-start.2) | copy-done | bytes 262168
  39.9 0.0 copy-start.3
  39.9 0.9 %copy-done.3 = f32[8,8,8,128]{3,2,1,0:T(8,128)S(1)} copy-done((f32[8,8,8,128]{3,2,1,0:T(8,128)S(1)}, f32[8,8,8,128]{3,2,1,0:T(8,128)}, u32[]{:S(2)}) %copy-start.3) | copy-done | bytes 262168
  40.9 27.5 %shard_map.87 = (f32[8,16,1024]{2,1,0:T(8,128)S(1)}, f32[1,256]{1,0:T(1,128)S(1)}) custom-call(f32[16,16,1024]{2,1,0:T(8,128)S(1)} %copy-done, f32[8,8,1024]{2,1,0:T(8,128)S(1)} %copy-done.1, f32[8,8,1024]{2,1,0:T(8,128)S(1)} %copy-done.2, f32[8,8,8,128]{3,2,1,0:T(8,128)S(1)} %copy-done.3), custom_call_target="tpu_custom_call" | custom-call | tf_op jit(solution)/shard_map/pallas_call | solution.py:384
  68.4 0.8 %copy.11 = f32[8,16,1024]{2,1,0:T(8,128)} copy(f32[8,16,1024]{2,1,0:T(8,128)S(1)} %get-tuple-element.12) | data formatting | bytes 1048576
  69.1 0.6 copy.12
Async XLA Ops:
  36.8 1.2 %copy-start = (f32[16,16,1024]{2,1,0:T(8,128)S(1)}, f32[16,16,1024]{2,1,0:T(8,128)}, u32[]{:S(2)}) copy-start(f32[16,16,1024]{2,1,0:T(8,128)} %get-tuple-element.6.y_in) | copy-start | bytes 3145732
  38.0 0.9 %copy-start.1 = (f32[8,8,1024]{2,1,0:T(8,128)S(1)}, f32[8,8,1024]{2,1,0:T(8,128)}, u32[]{:S(2)}) copy-start(f32[8,8,1024]{2,1,0:T(8,128)} %get-tuple-element.7.up_in) | copy-start | bytes 786436
  39.0 0.9 %copy-start.2 = (f32[8,8,1024]{2,1,0:T(8,128)S(1)}, f32[8,8,1024]{2,1,0:T(8,128)}, u32[]{:S(2)}) copy-start(f32[8,8,1024]{2,1,0:T(8,128)} %get-tuple-element.8.down_in) | copy-start | bytes 786436
  39.9 0.9 %copy-start.3 = (f32[8,8,8,128]{3,2,1,0:T(8,128)S(1)}, f32[8,8,8,128]{3,2,1,0:T(8,128)}, u32[]{:S(2)}) copy-start(f32[8,8,8,128]{3,2,1,0:T(8,128)} %get-tuple-element.9.r_in) | copy-start | bytes 786436

commit v2 on v1

v2 whole, which is shorter than its diff:
```python
import math

import jax
import jax.numpy as jnp
from jax import lax
from jax.experimental import pallas as pl
from jax.experimental.pallas import tpu as pltpu
from jax.sharding import PartitionSpec as P

SIGMA2 = 0.9 * 0.9
INV = 1.0 / SIGMA2
NORMAL = 1.0 / (0.9 * math.sqrt(2.0 * math.pi))
F32 = jnp.float32
BF16 = jnp.bfloat16
NT = (((1,), (1,)), ((), ()))
NN = (((1,), (0,)), ((), ()))
MESH = pl.DeviceIdType.MESH
TILE = 256


def iota(shape, dim):
    return lax.broadcasted_iota(jnp.int32, shape, dim)


def slot(row):
    return row - 4 if row >= 4 else row + 12


def slot_x(row):
    return row - 4 if row >= 4 else (row + 11 if row else 15)


def dense_taps(cell, frac, scale, out, tile, place, exact=False):
    u = cell.astype(F32) + (frac - 4.0)
    up = jnp.exp(u * INV)
    down = jnp.exp(u * (-INV))
    mid = jnp.exp(u * u * (-0.5 * INV)) * scale
    r = place(8)
    out[tile, 8 * r : 8 * r + 8, :] = mid
    below = [cell <= j for j in range(7)]
    p, q = mid, mid
    for k in range(1, 8):
        step = math.exp(-(2 * k - 1) * 0.5 * INV)
        p = p * (up * step) if exact else p * up
        q = q * (down * step) if exact else q * down
        r = place(8 + k)
        out[tile, 8 * r : 8 * r + 8, :] = jnp.where(below[k - 1], 0.0, p)
        r = place(8 - k)
        out[tile, 8 * r : 8 * r + 8, :] = jnp.where(below[7 - k], q, 0.0)


def crossed(x, y, tile, b):
    yy = y[tile, pl.ds(b, 16, stride=8), :].astype(BF16)
    parts = []
    for a in range(15):
        x8 = x[tile, pl.ds(a * 8 + b, 8, stride=0), :]
        parts.append(jnp.concatenate([x8, x8], 0).astype(BF16) * yy)
    return jnp.concatenate(parts + [jnp.zeros((16, 128), BF16)], 0)


def sincos(q, extent):
    eighth = extent // 8
    s = q + eighth
    quad = (s >> (extent.bit_length() - 3)) & 3
    r = ((s & (2 * eighth - 1)) - eighth).astype(F32) * (2.0 * math.pi / extent)
    r2 = r * r
    sin = r * (1.0 + r2 * (-1 / 6 + r2 * (1 / 120 + r2 * (-1 / 5040 + r2 * (1 / 362880)))))
    cos = 1.0 + r2 * (-0.5 + r2 * (1 / 24 + r2 * (-1 / 720 + r2 * (1 / 40320 + r2 * (-1 / 3628800)))))
    odd = (quad & 1) == 1
    c = jnp.where(odd, sin, cos)
    s = jnp.where(odd, cos, sin)
    c = jnp.where((quad == 1) | (quad == 2), -c, c)
    s = jnp.where(quad >= 2, -s, s)
    return c, s


def split(v):
    hi = v.astype(BF16)
    return hi, (v - hi.astype(F32)).astype(BF16)


def mm(a, b, dims=NN):
    return lax.dot_general(a, b, dims, preferred_element_type=F32)


def fused_kernel(
    cnt, cell, frac, w, mh, mk, ml,
    dens, inten,
    packed, fx, fy, fz, ws, xa, ya, za, xb, yb, zb, inner, edge, tab_hi, tab_lo, zsum, tt, d_hi, d_lo,
    amps, q, up_buf, down_buf, up_got, down_got, right_got, left_got, got1, part, got2,
    s1, g1, s2, g2, up_s, up_g, down_s, down_g, right_s, right_g, left_s, left_g,
):
    nx, ny = lax.axis_size("gx"), lax.axis_size("gy")
    me_x, me_y = lax.axis_index("gx"), lax.axis_index("gy")
    remote = nx > 1
    if remote:
        barrier = pltpu.get_barrier_semaphore()

        def greet_y(d, _):
            pl.semaphore_signal(barrier, inc=1, device_id=(me_x, (me_y + d) % ny), device_id_type=MESH)
            return 0

        def greet_x(d, _):
            pl.semaphore_signal(barrier, inc=1, device_id=((me_x + d) % nx, me_y), device_id_type=MESH)
            return 0

        lax.fori_loop(1, ny, greet_y, 0)
        lax.fori_loop(1, nx, greet_x, 0)

    def first(d, v):
        to = (me_y + d) % ny
        two = pl.ds(2 * v, 2)
        return pltpu.make_async_remote_copy(
            amps.at[to, two], got1.at[d, two], s1.at[v, d], g1.at[v, d], device_id=(me_x, to), device_id_type=MESH
        )

    def second(d):
        to = (me_x + d) % nx
        return pltpu.make_async_remote_copy(
            part.at[to // 2], got2.at[d], s2.at[d], g2.at[d], device_id=(to, me_y), device_id_type=MESH
        )

    def piece(src, dst, ss, gs, t, to):
        z = pl.ds(pl.multiple_of(t * TILE, TILE), TILE)
        return pltpu.make_async_remote_copy(
            src.at[:, :, z], dst.at[:, :, z], ss.at[t], gs.at[t], device_id=to, device_id_type=MESH
        )

    def ups(t):
        return piece(up_buf, up_got, up_s, up_g, t, (me_x, (me_y + 1) % ny))

    def downs(t):
        return piece(down_buf, down_got, down_s, down_g, t, (me_x, (me_y + ny - 1) % ny))

    def rights(t):
        return piece(q.at[pl.ds(8, 4)], right_got, right_s, right_g, t, ((me_x + 1) % nx, me_y))

    def lefts(t):
        return piece(q.at[pl.ds(12, 3)], left_got, left_s, left_g, t, ((me_x + nx - 1) % nx, me_y))

    def pieces(fn, out):
        for t in range(9):
            if t < 8:
                v = fn(t // 4, 128 * (t % 4), 128)
            else:
                v = jnp.concatenate([fn(0, 512, 64), fn(1, 512, 64)], 0)
            out[t] = v.T

    pieces(lambda c, s, n: cell[0, c, s : s + n] + cell[1, c, s : s + n] * 8 + cell[2, c, s : s + n] * 64, packed)
    for d, o in ((0, fx), (1, fy), (2, fz)):
        pieces(lambda c, s, n: frac[d, c, s : s + n], o)

    def weigh(c, s, n):
        taken = iota((n, 128), 0) + s < cnt[c : c + 1, :]
        return jnp.where(taken, w[c, s : s + n] * NORMAL, 0.0)

    pieces(weigh, ws)
    for o in (ya, za, yb, zb):
        for t in range(9):
            o[t, 96:104, :] = jnp.zeros((8, 128), F32)

    row8 = iota((8, 128), 0)
    lcol = jnp.concatenate([ml[v // 2] + (row8 + 8 * (v % 2) - 8) for v in range(16)], 0)
    c0, s0 = sincos((lcol * iota((128, 128), 1)) & 1023, 1024)
    cw, sw = sincos((lcol * 128) & 1023, 1024)
    for t in range(8):
        for half, v in ((0, c0), (1, -s0)):
            hi, lo = split(v)
            tab_hi[128 * half : 128 * half + 128, 128 * t : 128 * t + 128] = hi
            tab_lo[128 * half : 128 * half + 128, 128 * t : 128 * t + 128] = lo
        c0, s0 = c0 * cw - s0 * sw, s0 * cw + c0 * sw
    zsum[...] = jnp.zeros_like(zsum)

    def dense(g, t, taps):
        gs = pl.ds(pl.multiple_of(g * 8, 8), 8)
        p = packed[t, gs, :]
        dense_taps(p & 7, fx[t, gs, :], 1.0, taps[0], t, slot_x)
        dense_taps((p >> 3) & 7, fy[t, gs, :], 1.0, taps[1], t, slot)
        dense_taps(p >> 6, fz[t, gs, :], ws[t, gs, :], taps[2], t, slot, exact=True)

    lane16 = iota((16, 128), 1)

    def group(g, taps):
        xs, ys, zs = taps
        for t in (8, 0, 2, 4, 6):
            dense(g, t, taps)
            if t < 8:
                dense(g, t + 1, taps)
            for b in range(8):
                base = pl.multiple_of(g * 64 + b * 8, 8)
                here, there = pl.ds(base, 8), pl.ds(base + 8, 8)
                if t == 8:
                    zt = zs[8, pl.ds(b, 16, stride=8), :]
                    zm = jnp.concatenate([jnp.where(lane16 < 64, zt, 0.0), jnp.where(lane16 < 64, 0.0, zt)], 0)
                    f = mm(zm.astype(BF16), crossed(xs, ys, 8, b), NT)
                    for c in range(2):
                        inner[c, here, :] = f[16 * c : 16 * c + 8]
                        edge[c, there, :] = f[16 * c + 8 : 16 * c + 16]
                else:
                    zz = jnp.concatenate([zs[t + e, pl.ds(b, 16, stride=8), :] for e in (0, 1)], 1).astype(BF16)
                    cc = jnp.concatenate([crossed(xs, ys, t + e, b) for e in (0, 1)], 1)
                    f = mm(zz, cc, NT)
                    inner[t // 4, here, :] += f[0:8]
                    edge[t // 4, there, :] += f[8:16]

    taps_a, taps_b = (xa, ya, za), (xb, yb, zb)

    def groups(i, _):
        group((2 * i + 15) & 15, taps_a)
        group((2 * i) & 15, taps_b)
        return 0

    low256 = (iota((TILE, 256), 0) & 7) < 4
    lane = iota((8, 256), 1)
    k2 = jnp.zeros((8, 256), F32)
    for row in range(1, 16):
        square = float((row - 8) ** 2)
        k2 = k2 + jnp.where((lane >> 4) == slot_x(row), square, 0.0) + jnp.where((lane & 15) == slot(row), square, 0.0)
    gain = jnp.exp(k2 * (-0.5 * INV)) * (NORMAL * NORMAL)
    low = iota((8, TILE), 0) < 4

    def density_tile(t):
        z0 = pl.multiple_of(t * TILE, TILE)
        z = pl.ds(z0, TILE)
        spread = lambda v: jnp.concatenate([v] * (TILE // 8), 0)
        for c in range(2):
            beyond = jnp.where(low256, edge[c, z, :], edge[c, pl.ds(z0 + 16, TILE), :])
            d = (inner[c, z, :] + beyond) * spread(gain)
            tt[c] = d.T
            hi, lo = split(d)
            d_hi[...] = hi
            d_lo[...] = lo
            th = tab_hi[:, z]
            tl = tab_lo[:, z]
            zsum[c] += mm(th, d_hi[...]) + mm(th, d_lo[...]) + mm(tl, d_hi[...])
        for k in range(8):
            tops, bottoms = [], []
            for a in (2 * k, 2 * k + 1):
                in0, out0 = tt[0, 16 * a : 16 * a + 8, :], tt[0, 16 * a + 8 : 16 * a + 16, :]
                in1, out1 = tt[1, 16 * a : 16 * a + 8, :], tt[1, 16 * a + 8 : 16 * a + 16, :]
                q[a, 0:8, z] = in0 + jnp.where(low, 0.0, out1)
                q[a, 8:16, z] = in1 + jnp.where(low, out0, 0.0)
                tops.append(out1)
                bottoms.append(out0)
            up_buf[k, :, z] = jnp.where(low, tops[0], pltpu.roll(tops[1], 4, 0))
            down_buf[k, :, z] = jnp.where(low, pltpu.roll(bottoms[0], 4, 0), bottoms[1])

    def fold_y(t):
        z = pl.ds(pl.multiple_of(t * TILE, TILE), TILE)
        for k in (4, 5, 6, 7, 0, 1, 2, 3):
            a = 2 * k
            u, d = up_got[k, :, z], down_got[k, :, z]
            q[a, 0:8, z] += jnp.where(low, u, 0.0)
            q[a + 1, 0:8, z] += jnp.where(low, pltpu.roll(u, 4, 0), 0.0)
            q[a, 8:16, z] += jnp.where(low, 0.0, pltpu.roll(d, 4, 0))
            q[a + 1, 8:16, z] += jnp.where(low, 0.0, d)

    def pass_on(t):
        if remote:
            ups(t).wait()
            downs(t).wait()
        fold_y(t)
        if remote:
            rights(t).start()
            lefts(t).start()

    def tiles(t, _):
        lax.fori_loop(jnp.where(t == 0, 0, 2 * t + 1), jnp.where(t == 3, 8, 2 * t + 3), groups, 0)

        @pl.when(t == 0)
        def _():
            for c in range(2):
                edge[c, 0:8, :] = edge[c, 1024:1032, :]

        @pl.when(t == 3)
        def _():
            for c in range(2):
                edge[c, 1032:1040, :] = edge[c, 8:16, :]

        density_tile(t)
        if remote:

            @pl.when(t == 0)
            def _():
                pl.semaphore_wait(barrier, nx + ny - 2)

            ups(t).start()
            downs(t).start()

        @pl.when(t > 0)
        def _():
            pass_on(t - 1)

        return 0

    lax.fori_loop(0, 4, tiles, 0)

    x0 = me_x * 8
    y0 = me_y * 16
    n = iota((16, 256), 1)
    ip = (n & 63) >> 2
    ni = (ip & 1) * 8 + (ip >> 1) - 8
    nj = (n >> 6) * 4 + (n & 3) - 8
    off = iota((16, 256), 0)
    off_x = jnp.where(off < 12, off, off - 15)
    off_y = jnp.where(off < 12, off, off - 16)
    lane_low = iota((16, 128), 1) < 64

    def pair(v, _):
        us = []
        for e in range(2):
            win = 2 * v + e
            hx = mh[win] + ni
            ky = mk[win] + nj
            xr, xi = sincos((hx * (x0 + off_x)) & 127, 128)
            yr, yi = sincos((ky * (y0 + off_y)) & 127, 128)
            pr, pi = sincos((ky[0:1] * 8) & 127, 128)
            mr, mi = [], []
            for a in range(16):
                mr.append(xr[a : a + 1] * yr - xi[a : a + 1] * yi)
                mi.append(-(xr[a : a + 1] * yi + xi[a : a + 1] * yr))
            mrh, mrl = split(jnp.concatenate(mr, 0))
            mih, mil = split(jnp.concatenate(mi, 0))
            rows = [
                zsum[c, pl.ds(pl.multiple_of(128 * half + win * 16, 16), 16), :] for c in (0, 1) for half in (0, 1)
            ]
            zh, zl = split(jnp.concatenate(rows, 0))
            A = mm(zh, mrh) + mm(zl, mrh) + mm(zh, mrl)
            B = mm(zh, mih) + mm(zl, mih) + mm(zh, mil)
            re0, im0 = A[0:16] - B[16:32], A[16:32] + B[0:16]
            re1, im1 = A[32:48] - B[48:64], A[48:64] + B[32:48]
            us.append((re0 + re1 * pr + im1 * pi, im0 + im1 * pr - re1 * pi))
        rows = []
        for jh in range(4):
            for half in range(2):
                a0 = us[0][half][:, 128 * (jh // 2) : 128 * (jh // 2) + 128]
                a1 = us[1][half][:, 128 * (jh // 2) : 128 * (jh // 2) + 128]
                if jh % 2 == 0:
                    rows.append(jnp.where(lane_low, a0, pltpu.roll(a1, 64, 1)))
                else:
                    rows.append(jnp.where(lane_low, pltpu.roll(a0, 64, 1), a1))
        tr = jnp.concatenate(rows, 0).T
        for e in range(2):
            for il in range(8):
                amps[il, 2 * v + e] = tr[64 * e + 8 * il : 64 * e + 8 * il + 8]
        if remote:

            def send(d, _):
                first(d, v).start()
                return 0

            lax.fori_loop(1, ny, send, 0)
        return 0

    lax.fori_loop(0, 4, pair, 0)
    pass_on(3)

    if not remote:
        dens[...] = q[0:8]
        inten[...] = amps[0, 0, 0:1, :]
        return

    def finish_first(i, _):
        first(1 + i // 4, i % 4).wait()
        return 0

    lax.fori_loop(0, 4 * (ny - 1), finish_first, 0)
    part[...] = amps[me_y] + lax.fori_loop(2, ny, lambda d, s: s + got1[d], got1[1])

    def send_second(d, _):
        second(d).start()
        return 0

    def finish_second(d, _):
        second(d).wait()
        return 0

    lax.fori_loop(1, nx, send_second, 0)
    lax.fori_loop(1, nx, finish_second, 0)
    total = part[me_x // 2] + lax.fori_loop(2, nx, lambda d, s: s + got2[d], got2[1])
    odd = (iota((8, 128), 0) * 0 + me_x % 2) == 1
    mine = jnp.where(odd, pltpu.roll(total, 4, 0), total)
    power = mine * mine
    power = power + pltpu.roll(power, 112, 1)
    n = iota((128, 256), 1)
    pick = (iota((128, 256), 0) == (n >> 6) * 32 + (n & 15)).astype(F32)
    wide = lax.dot_general(power, pick, NN, precision=lax.Precision.HIGHEST, preferred_element_type=F32)
    keep = iota((8, 256), 0) == ((iota((8, 256), 1) >> 4) & 3)
    inten[...] = jnp.sum(jnp.where(keep, wide, 0.0), axis=0, keepdims=True) * (1.0 / 16777216.0)

    for t in range(4):
        z = slice(t * TILE, t * TILE + TILE)
        rights(t).wait()
        lefts(t).wait()
        dens[0:4, :, z] = q[0:4, :, z] + right_got[:, :, z]
        dens[4:5, :, z] = q[4:5, :, z]
        dens[5:8, :, z] = q[5:8, :, z] + left_got[:, :, z]


def local(cell, frac, w, cnt, mh, mk, ml):
    cell = jnp.swapaxes(cell, 2, 3)
    frac = jnp.swapaxes(frac, 2, 3)
    w = jnp.swapaxes(w, 1, 2)
    vm = pl.BlockSpec(memory_space=pltpu.VMEM)
    sm = pl.BlockSpec(memory_space=pltpu.SMEM)
    sd = jax.ShapeDtypeStruct
    vmem = pltpu.VMEM
    dma = pltpu.SemaphoreType.DMA
    multi = lax.axis_size("gx") > 1
    return pl.pallas_call(
        fused_kernel,
        out_shape=(sd((8, 16, 1024), F32), sd((1, 256 if multi else 128), F32)),
        in_specs=[vm] * 4 + [sm] * 3,
        out_specs=(vm, vm),
        scratch_shapes=[vmem((9, 128, 128), jnp.int32)]
        + [vmem((9, 128, 128), F32)] * 10
        + [
            vmem((2, 1024, 256), F32),
            vmem((2, 1040, 256), F32),
            vmem((256, 1024), BF16),
            vmem((256, 1024), BF16),
            vmem((2, 256, 256), F32),
            vmem((2, 256, TILE), F32),
            vmem((TILE, 256), BF16),
            vmem((TILE, 256), BF16),
            vmem((8, 8, 8, 128), F32),
            vmem((16, 16, 1024), F32),
            vmem((8, 8, 1024), F32),
            vmem((8, 8, 1024), F32),
            vmem((8, 8, 1024), F32),
            vmem((8, 8, 1024), F32),
            vmem((4, 16, 1024), F32),
            vmem((3, 16, 1024), F32),
            vmem((8, 8, 8, 128), F32),
            vmem((8, 8, 128), F32),
            vmem((16, 8, 128), F32),
            dma((4, 8)), dma((4, 8)), dma((16,)), dma((16,)),
        ]
        + [dma((4,))] * 8,
        compiler_params=pltpu.CompilerParams(
            collective_id=0 if multi else None, has_side_effects=True, vmem_limit_bytes=60 * 2**20
        ),
    )(cnt, cell, frac, w, mh, mk, ml)


def shards(atom_cell, atom_frac, atom_weight, block_count, miller_h, miller_k, miller_l):
    return local(atom_cell[:, 0], atom_frac[:, 0], atom_weight[0], block_count[0], miller_h, miller_k, miller_l)


def solution(mesh):
    in_specs = (
        P(None, "gx", "gy", None, None),
        P(None, "gx", "gy", None, None),
        P("gx", "gy", None, None),
        P("gx", "gy", None),
        P(),
        P(),
        P(),
    )
    out_specs = (P("gx", "gy", None), P(("gx", "gy"), None))
    return jax.shard_map(shards, mesh=mesh, in_specs=in_specs, out_specs=out_specs, check_vma=False)
```

time: 70 us -> 54.5 us (0.78)
  Pallas kernels: 63.6 us -> 50.6 us
  local copies, waits for them, and re-layouts: 5.43 us -> 3.08 us
    pallas_call x2 -> x1, Pallas kernels: 63.6 us -> 50.6 us  [local(): pl.pallas_call(fused_kernel, out_shape=(sd((8, 16, 1024), F32), sd((1, 25...]
    unnamed x10 -> x2, local copies, waits for them, and re-layouts: 5.43 us -> 3.08 us
where the time goes in v2:
time: 54.5 us; the launch traced here: 54.3 us
  Pallas kernels  50.6 us (93%)
  local copies, waits for them, and re-layouts  3.08 us (6%)
  between operations  0.64 us (1%)
    pallas_call x1, Pallas kernels, local(): pl.pallas_call(fused_kernel, out_shape=(sd((8, 16, 1024), F32), sd((1, 25...  50.6 us
    unnamed x2, local copies, waits for them, and re-layouts  3.08 us

profile of v2, /device:TPU:1, one launch (start us, length us, event | category | flops | bytes accessed | tf_op | source)
XLA Modules:
  0.0 54.3 jit_solution(4860749078375568819)
XLA Ops:
  0.6 50.6 %shard_map.86 = (f32[8,16,1024]{2,1,0:T(8,128)}, f32[1,256]{1,0:T(1,128)}) custom-call(s32[2,128]{1,0:T(2,128)} %bitcast.13, s32[3,2,576,128]{3,2,1,0:T(8,128)} %bitcast.10, f32[3,2,576,128]{3,2,1,0:T(8,128)} %bitcast.11, f32[2,576,128]{2,1,0:T(8,128)} %bitcast.12, s32[8]{0:T(128)} %mh.1, s32[8]{0:T(128)} %mk.1, s32[8]{0:T(128)} %ml.1), custom_call_target="tpu_custom_call" | custom-call | tf_op jit(solution)/shard_map/pallas_call | solution.py:410
  51.2 1.9 %copy.11 = f32[8,16,1024]{2,1,0:T(8,128)} copy(f32[8,16,1024]{2,1,0:T(8,128)} %get-tuple-element.4) | data formatting | bytes 1048576
  53.1 1.2 %copy.12 = f32[1,256]{1,0:T(1,128)} copy(f32[1,256]{1,0:T(1,128)} %get-tuple-element.5) | data formatting | bytes 2048

commit v3 on v2

--- a/solution.py
+++ b/solution.py
@@ -84,15 +84,21 @@
 
 
 def fused_kernel(
-    cnt, cell, frac, w, mh, mk, ml,
+    cnt, cell_in, frac_in, w_in, mh, mk, ml,
     dens, inten,
-    packed, fx, fy, fz, ws, xa, ya, za, xb, yb, zb, inner, edge, tab_hi, tab_lo, zsum, tt, d_hi, d_lo,
+    cell, frac, w, in_sem,
+    packed, fx, fy, fz, ws, xa, ya, za, xb, yb, zb, side_a, side_b, inner, edge, tab_hi, tab_lo, zsum, tt, d_hi, d_lo,
     amps, q, up_buf, down_buf, up_got, down_got, right_got, left_got, got1, part, got2,
     s1, g1, s2, g2, up_s, up_g, down_s, down_g, right_s, right_g, left_s, left_g,
 ):
     nx, ny = lax.axis_size("gx"), lax.axis_size("gy")
     me_x, me_y = lax.axis_index("gx"), lax.axis_index("gy")
     remote = nx > 1
+    loads = [pltpu.make_async_copy(cell_in, cell, in_sem.at[0])]
+    loads += [pltpu.make_async_copy(frac_in.at[d], frac.at[d], in_sem.at[1 + d]) for d in range(3)]
+    loads += [pltpu.make_async_copy(w_in, w, in_sem.at[4])]
+    for load in loads:
+        load.start()
     if remote:
         barrier = pltpu.get_barrier_semaphore()
 
@@ -137,27 +143,6 @@
 
     def lefts(t):
         return piece(q.at[pl.ds(12, 3)], left_got, left_s, left_g, t, ((me_x + nx - 1) % nx, me_y))
-
-    def pieces(fn, out):
-        for t in range(9):
-            if t < 8:
-                v = fn(t // 4, 128 * (t % 4), 128)
-            else:
-                v = jnp.concatenate([fn(0, 512, 64), fn(1, 512, 64)], 0)
-            out[t] = v.T
-
-    pieces(lambda c, s, n: cell[0, c, s : s + n] + cell[1, c, s : s + n] * 8 + cell[2, c, s : s + n] * 64, packed)
-    for d, o in ((0, fx), (1, fy), (2, fz)):
-        pieces(lambda c, s, n: frac[d, c, s : s + n], o)
-
-    def weigh(c, s, n):
-        taken = iota((n, 128), 0) + s < cnt[c : c + 1, :]
-        return jnp.where(taken, w[c, s : s + n] * NORMAL, 0.0)
-
-    pieces(weigh, ws)
-    for o in (ya, za, yb, zb):
-        for t in range(9):
-            o[t, 96:104, :] = jnp.zeros((8, 128), F32)
 
     row8 = iota((8, 128), 0)
     lcol = jnp.concatenate([ml[v // 2] + (row8 + 8 * (v % 2) - 8) for v in range(16)], 0)
@@ -171,6 +156,40 @@
         c0, s0 = c0 * cw - s0 * sw, s0 * cw + c0 * sw
     zsum[...] = jnp.zeros_like(zsum)
 
+    for o in (ya, za, yb, zb):
+        for t in range(9):
+            o[t, 96:104, :] = jnp.zeros((8, 128), F32)
+
+    def pieces(fn, out):
+        for t in range(9):
+            if t < 8:
+                v = fn(t // 4, 128 * (t % 4), 128)
+            else:
+                v = jnp.concatenate([fn(0, 512, 64), fn(1, 512, 64)], 0)
+            out[t] = v.T
+
+    loads[0].wait()
+    pieces(lambda c, s, n: cell[0, c, s : s + n] + cell[1, c, s : s + n] * 8 + cell[2, c, s : s + n] * 64, packed)
+    for d, o in ((0, fx), (1, fy), (2, fz)):
+        loads[1 + d].wait()
+        pieces(lambda c, s, n: frac[d, c, s : s + n], o)
+
+    def weigh(c, s, n):
+        taken = iota((n, 128), 0) + s < cnt[c : c + 1, :]
+        return jnp.where(taken, w[c, s : s + n] * NORMAL, 0.0)
+
+    loads[4].wait()
+    pieces(weigh, ws)
+    x0 = me_x * 8
+    y0 = me_y * 16
+    n = iota((16, 256), 1)
+    ip = (n & 63) >> 2
+    ni = (ip & 1) * 8 + (ip >> 1) - 8
+    nj = (n >> 6) * 4 + (n & 3) - 8
+    off = iota((16, 256), 0)
+    off_x = jnp.where(off < 12, off, off - 15)
+    off_y = jnp.where(off < 12, off, off - 16)
+
     def dense(g, t, taps):
         gs = pl.ds(pl.multiple_of(g * 8, 8), 8)
         p = packed[t, gs, :]
@@ -180,34 +199,46 @@
 
     lane16 = iota((16, 128), 1)
 
-    def group(g, taps):
+    def group(g, taps, side):
         xs, ys, zs = taps
-        for t in (8, 0, 2, 4, 6):
+        for t in range(9):
             dense(g, t, taps)
-            if t < 8:
-                dense(g, t + 1, taps)
-            for b in range(8):
-                base = pl.multiple_of(g * 64 + b * 8, 8)
-                here, there = pl.ds(base, 8), pl.ds(base + 8, 8)
-                if t == 8:
-                    zt = zs[8, pl.ds(b, 16, stride=8), :]
-                    zm = jnp.concatenate([jnp.where(lane16 < 64, zt, 0.0), jnp.where(lane16 < 64, 0.0, zt)], 0)
-                    f = mm(zm.astype(BF16), crossed(xs, ys, 8, b), NT)
-                    for c in range(2):
-                        inner[c, here, :] = f[16 * c : 16 * c + 8]
-                        edge[c, there, :] = f[16 * c + 8 : 16 * c + 16]
-                else:
-                    zz = jnp.concatenate([zs[t + e, pl.ds(b, 16, stride=8), :] for e in (0, 1)], 1).astype(BF16)
-                    cc = jnp.concatenate([crossed(xs, ys, t + e, b) for e in (0, 1)], 1)
-                    f = mm(zz, cc, NT)
-                    inner[t // 4, here, :] += f[0:8]
-                    edge[t // 4, there, :] += f[8:16]
+
+        def wide(ts, b):
+            zz = jnp.concatenate([zs[t, pl.ds(b, 16, stride=8), :] for t in ts], 1).astype(BF16)
+            return zz, jnp.concatenate([crossed(xs, ys, t, b) for t in ts], 1)
+
+        for b in range(8):
+            base = pl.multiple_of(g * 64 + b * 8, 8)
+            here, there = pl.ds(base, 8), pl.ds(base + 8, 8)
+            zt = zs[8, pl.ds(b, 16, stride=8), :]
+            zm = jnp.concatenate([jnp.where(lane16 < 64, zt, 0.0), jnp.where(lane16 < 64, 0.0, zt)], 0)
+            zz, cc = wide((4, 5), b)
+            st = mm(cc, zz, NT)
+            fm = mm(zm.astype(BF16), crossed(xs, ys, 8, b), NT)
+            zz, cc = wide((0, 1), b)
+            f = fm[0:16] + mm(zz, cc, NT)
+            zz, cc = wide((6, 7), b)
+            st = st + mm(cc, zz, NT)
+            zz, cc = wide((2, 3), b)
+            f = f + mm(zz, cc, NT)
+            side[:, 16 * b : 16 * b + 16] = st
+            inner[0, here, :] = f[0:8]
+            edge[0, there, :] = f[8:16]
+            inner[1, here, :] = fm[16:24]
+            edge[1, there, :] = fm[24:32]
+
+        tr = side[...].T
+        for b in range(8):
+            base = pl.multiple_of(g * 64 + b * 8, 8)
+            inner[1, pl.ds(base, 8), :] += tr[16 * b : 16 * b + 8]
+            edge[1, pl.ds(base + 8, 8), :] += tr[16 * b + 8 : 16 * b + 16]
 
     taps_a, taps_b = (xa, ya, za), (xb, yb, zb)
 
     def groups(i, _):
-        group((2 * i + 15) & 15, taps_a)
-        group((2 * i) & 15, taps_b)
+        group((2 * i + 15) & 15, taps_a, side_a)
+        group((2 * i) & 15, taps_b, side_b)
         return 0
 
     low256 = (iota((TILE, 256), 0) & 7) < 4
@@ -233,6 +264,9 @@
             th = tab_hi[:, z]
             tl = tab_lo[:, z]
             zsum[c] += mm(th, d_hi[...]) + mm(th, d_lo[...]) + mm(tl, d_hi[...])
+
+    def assemble(t):
+        z = pl.ds(pl.multiple_of(t * TILE, TILE), TILE)
         for k in range(8):
             tops, bottoms = [], []
             for a in (2 * k, 2 * k + 1):
@@ -278,43 +312,36 @@
                 edge[c, 1032:1040, :] = edge[c, 8:16, :]
 
         density_tile(t)
-        if remote:
-
-            @pl.when(t == 0)
+
+        @pl.when(t < 3)
+        def _():
+            assemble(t)
+            if remote:
+
+                @pl.when(t == 0)
+                def _():
+                    pl.semaphore_wait(barrier, nx + ny - 2)
+
+                ups(t).start()
+                downs(t).start()
+
+            @pl.when(t > 0)
             def _():
-                pl.semaphore_wait(barrier, nx + ny - 2)
-
-            ups(t).start()
-            downs(t).start()
-
-        @pl.when(t > 0)
-        def _():
-            pass_on(t - 1)
+                pass_on(t - 1)
 
         return 0
 
     lax.fori_loop(0, 4, tiles, 0)
 
-    x0 = me_x * 8
-    y0 = me_y * 16
-    n = iota((16, 256), 1)
-    ip = (n & 63) >> 2
-    ni = (ip & 1) * 8 + (ip >> 1) - 8
-    nj = (n >> 6) * 4 + (n & 3) - 8
-    off = iota((16, 256), 0)
-    off_x = jnp.where(off < 12, off, off - 15)
-    off_y = jnp.where(off < 12, off, off - 16)
     lane_low = iota((16, 128), 1) < 64
 
     def pair(v, _):
         us = []
         for e in range(2):
             win = 2 * v + e
-            hx = mh[win] + ni
-            ky = mk[win] + nj
-            xr, xi = sincos((hx * (x0 + off_x)) & 127, 128)
-            yr, yi = sincos((ky * (y0 + off_y)) & 127, 128)
-            pr, pi = sincos((ky[0:1] * 8) & 127, 128)
+            pr, pi = sincos(((mk[win] + nj[0:1]) * 8) & 127, 128)
+            xr, xi = sincos(((mh[win] + ni) * (x0 + off_x)) & 127, 128)
+            yr, yi = sincos(((mk[win] + nj) * (y0 + off_y)) & 127, 128)
             mr, mi = [], []
             for a in range(16):
                 mr.append(xr[a : a + 1] * yr - xi[a : a + 1] * yi)
@@ -353,9 +380,14 @@
         return 0
 
     lax.fori_loop(0, 4, pair, 0)
-    pass_on(3)
+    assemble(3)
+    if remote:
+        ups(3).start()
+        downs(3).start()
+    pass_on(2)
 
     if not remote:
+        pass_on(3)
         dens[...] = q[0:8]
         inten[...] = amps[0, 0, 0:1, :]
         return
@@ -365,7 +397,10 @@
         return 0
 
     lax.fori_loop(0, 4 * (ny - 1), finish_first, 0)
-    part[...] = amps[me_y] + lax.fori_loop(2, ny, lambda d, s: s + got1[d], got1[1])
+    own = amps[me_y]
+    for d in range(1, 8):
+        own = own + got1[d]
+    part[...] = own
 
     def send_second(d, _):
         second(d).start()
@@ -376,16 +411,19 @@
         return 0
 
     lax.fori_loop(1, nx, send_second, 0)
+    n = iota((128, 256), 1)
+    pick = (iota((128, 256), 0) == (n >> 6) * 32 + (n & 15)).astype(F32)
+    keep = iota((8, 256), 0) == ((iota((8, 256), 1) >> 4) & 3)
+    odd = (iota((8, 128), 0) * 0 + me_x % 2) == 1
+    pass_on(3)
     lax.fori_loop(1, nx, finish_second, 0)
-    total = part[me_x // 2] + lax.fori_loop(2, nx, lambda d, s: s + got2[d], got2[1])
-    odd = (iota((8, 128), 0) * 0 + me_x % 2) == 1
+    total = part[me_x // 2]
+    for d in range(1, 16):
+        total = total + got2[d]
     mine = jnp.where(odd, pltpu.roll(total, 4, 0), total)
     power = mine * mine
     power = power + pltpu.roll(power, 112, 1)
-    n = iota((128, 256), 1)
-    pick = (iota((128, 256), 0) == (n >> 6) * 32 + (n & 15)).astype(F32)
     wide = lax.dot_general(power, pick, NN, precision=lax.Precision.HIGHEST, preferred_element_type=F32)
-    keep = iota((8, 256), 0) == ((iota((8, 256), 1) >> 4) & 3)
     inten[...] = jnp.sum(jnp.where(keep, wide, 0.0), axis=0, keepdims=True) * (1.0 / 16777216.0)
 
     for t in range(4):
@@ -403,6 +441,7 @@
     w = jnp.swapaxes(w, 1, 2)
     vm = pl.BlockSpec(memory_space=pltpu.VMEM)
     sm = pl.BlockSpec(memory_space=pltpu.SMEM)
+    hbm = pl.BlockSpec(memory_space=pltpu.HBM)
     sd = jax.ShapeDtypeStruct
     vmem = pltpu.VMEM
     dma = pltpu.SemaphoreType.DMA
@@ -410,11 +449,19 @@
     return pl.pallas_call(
         fused_kernel,
         out_shape=(sd((8, 16, 1024), F32), sd((1, 256 if multi else 128), F32)),
-        in_specs=[vm] * 4 + [sm] * 3,
+        in_specs=[vm] + [hbm] * 3 + [sm] * 3,
         out_specs=(vm, vm),
-        scratch_shapes=[vmem((9, 128, 128), jnp.int32)]
+        scratch_shapes=[
+            vmem((3, 2, 576, 128), jnp.int32),
+            vmem((3, 2, 576, 128), F32),
+            vmem((2, 576, 128), F32),
+            dma((5,)),
+            vmem((9, 128, 128), jnp.int32),
+        ]
         + [vmem((9, 128, 128), F32)] * 10
         + [
+            vmem((256, 128), F32),
+            vmem((256, 128), F32),
             vmem((2, 1024, 256), F32),
             vmem((2, 1040, 256), F32),
             vmem((256, 1024), BF16),
@@ -438,7 +485,7 @@
         ]
         + [dma((4,))] * 8,
         compiler_params=pltpu.CompilerParams(
-            collective_id=0 if multi else None, has_side_effects=True, vmem_limit_bytes=60 * 2**20
+            collective_id=0 if multi else None, has_side_effects=True, vmem_limit_bytes=58 * 2**20
         ),
     )(cnt, cell, frac, w, mh, mk, ml)
 

time: 54.5 us -> 50.1 us (0.919)
  Pallas kernels: 50.6 us -> 46.2 us
    pallas_call x1, Pallas kernels: 50.6 us -> 46.2 us  [local(): pl.pallas_call(fused_kernel, out_shape=(sd((8, 16, 1024), F32), sd((1, 25...]
where the time goes in v3:
time: 50.1 us; the launch traced here: 49.9 us
  Pallas kernels  46.2 us (92%)
  local copies, waits for them, and re-layouts  3.08 us (6%)
  between operations  0.64 us (1%)
    pallas_call x1, Pallas kernels, local(): pl.pallas_call(fused_kernel, out_shape=(sd((8, 16, 1024), F32), sd((1, 25...  46.2 us
    unnamed x2, local copies, waits for them, and re-layouts  3.08 us

profile of v3, /device:TPU:1, one launch (start us, length us, event | category | flops | bytes accessed | tf_op | source)
XLA Modules:
  0.0 49.9 jit_solution(14640104372620746562)
XLA Ops:
  0.6 46.2 %shard_map.86 = (f32[8,16,1024]{2,1,0:T(8,128)}, f32[1,256]{1,0:T(1,128)}) custom-call(s32[2,128]{1,0:T(2,128)} %bitcast.13, s32[3,2,576,128]{3,2,1,0:T(8,128)} %bitcast.10, f32[3,2,576,128]{3,2,1,0:T(8,128)} %bitcast.11, f32[2,576,128]{2,1,0:T(8,128)} %bitcast.12, s32[8]{0:T(128)} %mh.1, s32[8]{0:T(128)} %mk.1, s32[8]{0:T(128)} %ml.1), custom_call_target="tpu_custom_call" | custom-call | tf_op jit(solution)/shard_map/pallas_call | solution.py:449
  46.8 1.9 %copy.11 = f32[8,16,1024]{2,1,0:T(8,128)} copy(f32[8,16,1024]{2,1,0:T(8,128)} %get-tuple-element.4) | data formatting | bytes 1048576
  48.7 1.2 %copy.12 = f32[1,256]{1,0:T(1,128)} copy(f32[1,256]{1,0:T(1,128)} %get-tuple-element.5) | data formatting | bytes 2048
